TPU v7x, 256 devices: a whole 4x4x8 slice. The times are simulated.
256 devices in a mesh: dp: 4 (over x), seq: 16 (over z, core), tensor: 4 (over y).
Axes of the slice: x: 4, y: 4, z: 8, core: 2. Of those that a mesh axis runs over, the one named last changes fastest.
Arguments:
- feature_in: bfloat16 [16, 2048, 512], P('dp', 'seq', 'tensor'), may hold values from -6 to 6
- conv_weight: bfloat16 [2, 512, 512], P(None, 'tensor'), may hold values from -0.1875 to 0.1875
- proj_weight: bfloat16 [512, 1920], P(None, 'tensor'), may hold values from -0.25 to 0.25
- mask_embed: bfloat16 [1920], P('tensor'), may hold values from -5 to 5
- pos_weight: bfloat16 [128, 16, 120, 120], P(('dp', 'seq'), 'tensor'), may hold values from -0.046875 to 0.046875
- final_weight: bfloat16 [1920, 1024], P('tensor'), may hold values from -0.125 to 0.125
- codebook: bfloat16 [2, 320, 512], replicated, may hold values from -6 to 6
- quant_weight: bfloat16 [1024, 1024], replicated, may hold values from -0.1875 to 0.1875
- mask_starts: int32 [16, 66], P('dp'), may hold values from 0 to 1014
- code_choice: int32 [16, 1024, 2], P(('dp', 'tensor'), 'seq'), may hold values from 0 to 319
- negative_ids: int32 [16, 1024, 100], P(('dp', 'tensor'), 'seq'), may hold values from 0 to 1023, as said below
Outputs:
- frame_loss: float32 [16, 1024], P(('dp', 'tensor'), 'seq')
Inputs may be any that keep to these rules, and one draw needn't show every extreme that they name: `negative_ids`: each entry names a frame of the same utterance other than the frame itself.
All inputs are finite; a program needn't handle non-finite values.
Results may differ from a plain program's by a relative error of at most 0.00065.
Values may be sent and summed in bfloat16 or wider, within the bound.
A program may use at most 128 MiB of HBM per device.

v0:
```python
import jax
import jax.numpy as jnp
from jax import lax
from jax.sharding import PartitionSpec as P

KERNEL = 128
MASK_LEN = 10
ln_eps = 1e-05
norm_eps = 1e-06
logit_temp = 0.1


def extended(block, sides, width):
    for axis, dim in sides:
        count = lax.axis_size(axis)
        forward = [(i, i + 1) for i in range(count - 1)]
        backward = [(target, source) for source, target in forward]
        low = lax.ppermute(
            lax.slice_in_dim(block, block.shape[dim] - width, None, axis=dim), axis, forward
        )
        high = lax.ppermute(lax.slice_in_dim(block, 0, width, axis=dim), axis, backward)
        block = jnp.concatenate([low, block, high], axis=dim)
    return block


def make_targets(code_block, codebook, quant_weight):
    entries = codebook.shape[1]
    choices_row = jnp.arange(entries, dtype=jnp.int32)
    pieces = []
    for qgroup in range(codebook.shape[0]):
        onehot = (code_block[..., qgroup, None] == choices_row).astype(jnp.bfloat16)
        pieces.append(
            jnp.dot(onehot, codebook[qgroup], preferred_element_type=jnp.float32).astype(
                jnp.bfloat16
            )
        )
    codevec = jnp.concatenate(pieces, axis=-1)
    return jnp.dot(codevec, quant_weight, preferred_element_type=jnp.float32).astype(jnp.bfloat16)


def utterance_loss(context, own_targets, all_targets, neg_ids, is_masked):
    scores = jnp.einsum("fc,nc->fn", context, all_targets, preferred_element_type=jnp.float32)
    ctx_norm = jnp.einsum("fc,fc->f", context, context, preferred_element_type=jnp.float32)
    own_norm = jnp.einsum("fc,fc->f", own_targets, own_targets, preferred_element_type=jnp.float32)
    tgt_norm = jnp.einsum("nc,nc->n", all_targets, all_targets, preferred_element_type=jnp.float32)
    pos_dot = jnp.einsum("fc,fc->f", context, own_targets, preferred_element_type=jnp.float32)
    neg_dot = jnp.take_along_axis(scores, neg_ids, axis=1)
    neg_norm = tgt_norm[neg_ids]
    positive = pos_dot * lax.rsqrt((ctx_norm + norm_eps) * (own_norm + norm_eps)) / logit_temp
    negative = (
        neg_dot * lax.rsqrt((ctx_norm[:, None] + norm_eps) * (neg_norm + norm_eps)) / logit_temp
    )
    frame_loss = jnp.log(jnp.exp(positive) + jnp.sum(jnp.exp(negative), axis=-1)) - positive
    return jnp.where(is_masked, frame_loss, jnp.zeros_like(frame_loss))


def tap_sum(windows, running, tap_block, frames):
    count = tap_block.shape[0]
    joined_taps = max((d for d in range(1, 17) if count % d == 0))
    group_count, inner, outer = (tap_block.shape[1], tap_block.shape[2], tap_block.shape[3])

    def add_block(step, partial_value):
        base = step * joined_taps
        slabs = [
            lax.dynamic_slice_in_dim(windows, base + offset, frames, 1)
            for offset in range(joined_taps)
        ]
        joined = jnp.concatenate(slabs, axis=-1)
        taps = lax.dynamic_slice_in_dim(tap_block, base, joined_taps, 0)
        taps = jnp.transpose(taps, (1, 0, 2, 3)).reshape(group_count, joined_taps * inner, outer)
        return partial_value + jnp.einsum(
            "ufgi,gio->ufgo", joined, taps, preferred_element_type=jnp.float32
        )

    return lax.fori_loop(0, count // joined_taps, add_block, running)


def on_device(
    feature_in,
    conv_weight,
    proj_weight,
    mask_embed,
    pos_weight,
    final_weight,
    codebook,
    quant_weight,
    mask_starts,
    code_choice,
    negative_ids,
):
    utt_count, sample_rows, channels = feature_in.shape
    frames = sample_rows // 2
    frame_pairs = feature_in.reshape(utt_count, frames, 2 * channels)
    conv_term = jnp.dot(
        frame_pairs,
        conv_weight.reshape(2 * channels, conv_weight.shape[2]),
        preferred_element_type=jnp.float32,
    )
    summed = lax.psum(conv_term, "tensor")
    row_mean = jnp.mean(summed, axis=-1, keepdims=True)
    row_square = jnp.mean(summed * summed, axis=-1, keepdims=True)
    normed = (summed - row_mean) * lax.rsqrt(row_square - row_mean * row_mean + ln_eps)
    features = jax.nn.gelu(normed, approximate=False).astype(jnp.bfloat16)
    projected = jnp.dot(features, proj_weight, preferred_element_type=jnp.float32).astype(
        jnp.bfloat16
    )
    positions = (lax.axis_index("seq") * frames + jnp.arange(frames, dtype=jnp.int32))[
        None, :, None
    ]
    starts = mask_starts[:, None, :]
    masked = jnp.any((positions >= starts) & (positions < starts + MASK_LEN), axis=-1)
    hidden = jnp.where(masked[..., None], mask_embed[None, None, :], projected)
    padded = extended(hidden, (("seq", 1),), KERNEL // 2)
    group_count = pos_weight.shape[1]
    inner = pos_weight.shape[2]
    outer = pos_weight.shape[3]
    windows = padded.reshape(utt_count, padded.shape[1], group_count, inner)
    initial = jnp.zeros((utt_count, frames, group_count, outer), jnp.float32)
    conv_out = tap_sum(
        windows, initial, lax.all_gather(pos_weight, ("dp", "seq"), axis=0, tiled=True), frames
    )
    conv_out = conv_out.reshape(utt_count, frames, group_count * outer)
    mixed = (hidden.astype(jnp.float32) + jax.nn.gelu(conv_out, approximate=False)).astype(
        jnp.bfloat16
    )
    utt_rows = utt_count // lax.axis_size("tensor")
    context = lax.psum_scatter(
        jnp.dot(mixed, final_weight, preferred_element_type=jnp.float32),
        "tensor",
        scatter_dimension=0,
        tiled=True,
    ).astype(jnp.bfloat16)
    own_targets = make_targets(code_choice, codebook, quant_weight)
    all_targets = lax.all_gather(own_targets, "seq", axis=1, tiled=True)
    is_masked = lax.dynamic_slice_in_dim(masked, lax.axis_index("tensor") * utt_rows, utt_rows, 0)
    return jax.vmap(utterance_loss)(context, own_targets, all_targets, negative_ids, is_masked)


def solution(mesh):
    return jax.shard_map(
        on_device,
        mesh=mesh,
        in_specs=(
            P("dp", "seq", "tensor"),
            P(None, "tensor", None),
            P(None, "tensor"),
            P("tensor"),
            P(("dp", "seq"), "tensor", None, None),
            P("tensor", None),
            P(),
            P(),
            P("dp", None),
            P(("dp", "tensor"), "seq", None),
            P(("dp", "tensor"), "seq", None),
        ),
        out_specs=P(("dp", "tensor"), "seq"),
        check_vma=False,
    )
```

profile of v0, /device:TPU:1, one launch (start us, length us, event | category | flops | bytes accessed | tf_op | source)
XLA Modules:
  0.0 506.4 jit_solution(2708013920155017598)
XLA Ops:
  12.7 48.5 %all-reduce.2.cloned.1.call-done = f32[4,64,512]{2,1,0:T(8,128)} async-done(((f32[4,64,512]{2,1,0:T(8,128)}), f32[4,64,512]{2,1,0:T(8,128)}) %all-reduce.2.cloned.1.call-update) | async-done | bytes 524304 | tf_op jit(solution)/shard_map/psum | solution.py:99
  65.0 5.1 %collective-permute-start = (bf16[4,64,480]{2,1,0:T(8,128)(2,1)S(1)}, bf16[4,64,480]{2,1,0:T(8,128)(2,1)S(1)}, u32[]{:S(2)}, u32[]{:S(2)}) collective-permute-start(bf16[4,64,480]{2,1,0:T(8,128)(2,1)S(1)} %fusion.1), channel_id=1, source_target_pairs={{0,4},{4,8},{8,12},{12,16},{16,20},{20,24},{24,28},{28,32},{32,36}... | collective-permute-start | bytes 737288 | tf_op jit(solution)/shard_map/ppermute | solution.py:18
  72.0 6.7 %collective-permute-done = bf16[4,64,480]{2,1,0:T(8,128)(2,1)S(1)} collective-permute-done((bf16[4,64,480]{2,1,0:T(8,128)(2,1)S(1)}, bf16[4,64,480]{2,1,0:T(8,128)(2,1)S(1)}, u32[]{:S(2)}, u32[]{:S(2)}) %collective-permute-start) | collective-permute-done | bytes 245792 | tf_op jit(solution)/shard_map/ppermute | solution.py:18
  78.8 4.0 collective-permute-done.1
  86.5 28.4 %all-gather.4.cloned.1.call-done = bf16[128,4,120,120]{3,2,1,0:T(8,128)(2,1)} async-done(((bf16[2,4,120,120]{3,2,1,0:T(8,128)(2,1)}), bf16[128,4,120,120]{3,2,1,0:T(8,128)(2,1)}) %all-gather.4.cloned.1.call-update) | async-done | bytes 14745616 | tf_op jit(solution)/shard_map/all_gather | solution.py:120
  114.9 222.5 %while.16 = (s32[]{:T(128)}, f32[4,64,4,120]{3,1,0,2:T(8,128)}, bf16[128,4,120,120]{3,2,1,0:T(8,128)(2,1)}, bf16[4,192,4,120]{3,1,0,2:T(8,128)(2,1)S(1)}, s32[]{...) while((s32[]{:T(128)}, f32[4,64,4,120]{3,1,0,2:T(8,128)}, ...), condition=%wide.region_5.6_spmd.clone, body=%wide.region_4.5_spmd.clone.sunk | while | flops 472105024 | bytes 34530440 | solution.py:75
  117.9 7.1 %concatenate.26 = bf16[4,64,4,1920]{3,1,0,2:T(8,128)(2,1)} concatenate(bf16[4,64,4,120]{3,1,0,2:T(8,128)(2,1)} %get-tuple-element.238, bf16[4,64,4,120]{3,1,0,2:T(8,128)(2,1)} %get-tuple-element.239, bf16[4,64,4,120]{3,1,0,2:T(8,128)(2,1)} %get-tuple-element.240, bf16[4,64,4,120]{3,1,0,2:T(8,128)(2,1)} %get-tuple-element.241, bf16[4,64,4,120]{3,1,0,2:T(8,128)(2,1)} %get-tuple-element.242, ...), dimensions={3} | concatenate | bytes 7864320 | tf_op jit(solution)/shard_map/while/body/eval_jaxpr/concatenate | solution.py:68
  128.0 4.4 copy.47
  132.5 4.6 reshape.312
  137.1 3.8 fusion.188
  144.8 7.1 %concatenate.26 = bf16[4,64,4,1920]{3,1,0,2:T(8,128)(2,1)} concatenate(bf16[4,64,4,120]{3,1,0,2:T(8,128)(2,1)} %get-tuple-element.238, bf16[4,64,4,120]{3,1,0,2:T(8,128)(2,1)} %get-tuple-element.239, bf16[4,64,4,120]{3,1,0,2:T(8,128)(2,1)} %get-tuple-element.240, bf16[4,64,4,120]{3,1,0,2:T(8,128)(2,1)} %get-tuple-element.241, bf16[4,64,4,120]{3,1,0,2:T(8,128)(2,1)} %get-tuple-element.242, ...), dimensions={3} | concatenate | bytes 7864320 | tf_op jit(solution)/shard_map/while/body/eval_jaxpr/concatenate | solution.py:68
  151.9 3.0 constant_dynamic-slice_fusion.19
  154.9 4.4 copy.47
  159.4 4.6 reshape.312
  164.0 3.8 fusion.188
  172.7 7.1 %concatenate.26 = bf16[4,64,4,1920]{3,1,0,2:T(8,128)(2,1)} concatenate(bf16[4,64,4,120]{3,1,0,2:T(8,128)(2,1)} %get-tuple-element.238, bf16[4,64,4,120]{3,1,0,2:T(8,128)(2,1)} %get-tuple-element.239, bf16[4,64,4,120]{3,1,0,2:T(8,128)(2,1)} %get-tuple-element.240, bf16[4,64,4,120]{3,1,0,2:T(8,128)(2,1)} %get-tuple-element.241, bf16[4,64,4,120]{3,1,0,2:T(8,128)(2,1)} %get-tuple-element.242, ...), dimensions={3} | concatenate | bytes 7864320 | tf_op jit(solution)/shard_map/while/body/eval_jaxpr/concatenate | solution.py:68
  182.9 4.4 copy.47
  187.3 4.6 reshape.312
  191.9 3.8 fusion.188
  200.7 7.1 %concatenate.26 = bf16[4,64,4,1920]{3,1,0,2:T(8,128)(2,1)} concatenate(bf16[4,64,4,120]{3,1,0,2:T(8,128)(2,1)} %get-tuple-element.238, bf16[4,64,4,120]{3,1,0,2:T(8,128)(2,1)} %get-tuple-element.239, bf16[4,64,4,120]{3,1,0,2:T(8,128)(2,1)} %get-tuple-element.240, bf16[4,64,4,120]{3,1,0,2:T(8,128)(2,1)} %get-tuple-element.241, bf16[4,64,4,120]{3,1,0,2:T(8,128)(2,1)} %get-tuple-element.242, ...), dimensions={3} | concatenate | bytes 7864320 | tf_op jit(solution)/shard_map/while/body/eval_jaxpr/concatenate | solution.py:68
  207.8 3.0 constant_dynamic-slice_fusion.19
  210.9 4.4 copy.47
  215.3 4.6 reshape.312
  219.9 3.8 fusion.188
  228.6 7.1 %concatenate.26 = bf16[4,64,4,1920]{3,1,0,2:T(8,128)(2,1)} concatenate(bf16[4,64,4,120]{3,1,0,2:T(8,128)(2,1)} %get-tuple-element.238, bf16[4,64,4,120]{3,1,0,2:T(8,128)(2,1)} %get-tuple-element.239, bf16[4,64,4,120]{3,1,0,2:T(8,128)(2,1)} %get-tuple-element.240, bf16[4,64,4,120]{3,1,0,2:T(8,128)(2,1)} %get-tuple-element.241, bf16[4,64,4,120]{3,1,0,2:T(8,128)(2,1)} %get-tuple-element.242, ...), dimensions={3} | concatenate | bytes 7864320 | tf_op jit(solution)/shard_map/while/body/eval_jaxpr/concatenate | solution.py:68
  238.8 4.4 copy.47
  243.2 4.6 reshape.312
  247.8 3.8 fusion.188
  256.5 7.1 %concatenate.26 = bf16[4,64,4,1920]{3,1,0,2:T(8,128)(2,1)} concatenate(bf16[4,64,4,120]{3,1,0,2:T(8,128)(2,1)} %get-tuple-element.238, bf16[4,64,4,120]{3,1,0,2:T(8,128)(2,1)} %get-tuple-element.239, bf16[4,64,4,120]{3,1,0,2:T(8,128)(2,1)} %get-tuple-element.240, bf16[4,64,4,120]{3,1,0,2:T(8,128)(2,1)} %get-tuple-element.241, bf16[4,64,4,120]{3,1,0,2:T(8,128)(2,1)} %get-tuple-element.242, ...), dimensions={3} | concatenate | bytes 7864320 | tf_op jit(solution)/shard_map/while/body/eval_jaxpr/concatenate | solution.py:68
  263.7 3.0 constant_dynamic-slice_fusion.19
  266.7 4.4 copy.47
  271.2 4.6 reshape.312
  275.7 3.8 fusion.188
  284.5 7.1 %concatenate.26 = bf16[4,64,4,1920]{3,1,0,2:T(8,128)(2,1)} concatenate(bf16[4,64,4,120]{3,1,0,2:T(8,128)(2,1)} %get-tuple-element.238, bf16[4,64,4,120]{3,1,0,2:T(8,128)(2,1)} %get-tuple-element.239, bf16[4,64,4,120]{3,1,0,2:T(8,128)(2,1)} %get-tuple-element.240, bf16[4,64,4,120]{3,1,0,2:T(8,128)(2,1)} %get-tuple-element.241, bf16[4,64,4,120]{3,1,0,2:T(8,128)(2,1)} %get-tuple-element.242, ...), dimensions={3} | concatenate | bytes 7864320 | tf_op jit(solution)/shard_map/while/body/eval_jaxpr/concatenate | solution.py:68
  291.6 3.0 constant_dynamic-slice_fusion.19
  294.7 4.4 copy.47
  299.1 4.6 reshape.312
  303.7 3.9 fusion.188
  312.5 7.1 %concatenate.26 = bf16[4,64,4,1920]{3,1,0,2:T(8,128)(2,1)} concatenate(bf16[4,64,4,120]{3,1,0,2:T(8,128)(2,1)} %get-tuple-element.238, bf16[4,64,4,120]{3,1,0,2:T(8,128)(2,1)} %get-tuple-element.239, bf16[4,64,4,120]{3,1,0,2:T(8,128)(2,1)} %get-tuple-element.240, bf16[4,64,4,120]{3,1,0,2:T(8,128)(2,1)} %get-tuple-element.241, bf16[4,64,4,120]{3,1,0,2:T(8,128)(2,1)} %get-tuple-element.242, ...), dimensions={3} | concatenate | bytes 7864320 | tf_op jit(solution)/shard_map/while/body/eval_jaxpr/concatenate | solution.py:68
  319.6 3.0 constant_dynamic-slice_fusion.19
  322.7 4.4 copy.47
  327.1 4.6 reshape.312
  331.7 3.8 fusion.188
  340.7 3.8 fusion.4
  347.1 19.4 %reduce-scatter.2.cloned.1.call-done = f32[1,64,1024]{2,1,0:T(8,128)} async-done(((f32[4,64,1024]{2,1,0:T(8,128)}), f32[1,64,1024]{2,1,0:T(8,128)}) %reduce-scatter.2.cloned.1.call-update) | async-done | bytes 262160 | tf_op jit(solution)/shard_map/reduce_scatter | solution.py:127
  369.3 41.1 %all-gather.6.cloned.1.call-done = bf16[1024,1024]{1,0:T(8,128)(2,1)} async-done(((bf16[64,1024]{1,0:T(8,128)(2,1)}), bf16[1024,1024]{1,0:T(8,128)(2,1)}) %all-gather.6.cloned.1.call-update) | async-done | bytes 2097168 | tf_op jit(solution)/shard_map/all_gather | solution.py:134
  412.7 48.5 %gather_fusion = f32[6400]{0:T(1024)S(1)} fusion(f32[1,64,1024]{2,1,0:T(8,128)S(1)} %convolution_bitcast_fusion, s32[6400]{0:T(1024)S(1)} %reshape.273), kind=kCustom, calls=%fused_computation | custom fusion | bytes 128000 | tf_op jit(solution)/shard_map/vmap(jit(take_along_axis))/gather | solution.py:47
  463.3 35.1 %gather_fusion.1 = f32[6400]{0:T(1024)S(1)} fusion(f32[1,1024]{1,0:T(1,128)S(1)} %bitcast.82, s32[6400]{0:T(1024)S(1)} %reshape.281), kind=kCustom, calls=%fused_computation.1 | custom fusion | bytes 102400 | tf_op jit(solution)/shard_map/vmap()/gather | solution.py:48
  (78 shorter events, 75.8 us)
Async XLA Ops:
  7.4 359.2 %copy-start = (bf16[1024,1024]{1,0:T(8,128)(2,1)S(1)}, bf16[1024,1024]{1,0:T(8,128)(2,1)}, u32[]{:S(2)}) copy-start(bf16[1024,1024]{1,0:T(8,128)(2,1)} %param.20) | copy-start | bytes 6291460
  7.4 53.8 %all-reduce.2.cloned.1.call-start = ((), (), s32[]{:S(2)}) async-start(), calls=%async_computation.1 | async-start | bytes 1048576 | tf_op jit(solution)/shard_map/psum | solution.py:99
  10.5 104.4 %all-gather.4.cloned.1.call-start = ((), (), s32[]{:S(2)}) async-start(), calls=%async_computation.2 | async-start | bytes 15974400 | tf_op jit(solution)/shard_map/all_gather | solution.py:120
  11.1 355.5 %reduce-scatter.2.cloned.1.call-start = ((), (), s32[]{:S(2)}) async-start(), calls=%async_computation.3 | async-start | bytes 1310720 | tf_op jit(solution)/shard_map/reduce_scatter | solution.py:127
  65.0 49.9 %copy-start.2 = (bf16[4,64,480]{2,1,0:T(8,128)(2,1)}, bf16[4,64,480]{2,1,0:T(8,128)(2,1)S(1)}, u32[]{:S(2)}) copy-start(bf16[4,64,480]{2,1,0:T(8,128)(2,1)S(1)} %fusion.1) | copy-start | bytes 737284
  65.0 13.7 %collective-permute-start = (bf16[4,64,480]{2,1,0:T(8,128)(2,1)S(1)}, bf16[4,64,480]{2,1,0:T(8,128)(2,1)S(1)}, u32[]{:S(2)}, u32[]{:S(2)}) collective-permute-start(bf16[4,64,480]{2,1,0:T(8,128)(2,1)S(1)} %fusion.1), channel_id=1, source_target_pairs={{0,4},{4,8},{8,12},{12,16},{16,20},{20,24},{24,28},{28,32},{32,36}... | collective-permute-start | bytes 737288 | tf_op jit(solution)/shard_map/ppermute | solution.py:18
  70.1 12.7 %collective-permute-start.1 = (bf16[4,64,480]{2,1,0:T(8,128)(2,1)S(1)}, bf16[4,64,480]{2,1,0:T(8,128)(2,1)}, u32[]{:S(2)}, u32[]{:S(2)}) collective-permute-start(bf16[4,64,480]{2,1,0:T(8,128)(2,1)S(1)} %fusion.1), channel_id=1, source_target_pairs={{4,0},{8,4},{12,8},{16,12},{20,16},{24,20},{28,24},{32,28},{36,32}... | collective-permute-start | bytes 737288 | tf_op jit(solution)/shard_map/ppermute | solution.py:21
  337.5 3.2 copy-start.3
  340.7 4.1 copy-start.5
  344.5 24.4 %copy-start.4 = (s32[1,64,100]{2,1,0:T(8,128)S(1)}, s32[1,64,100]{2,1,0:T(8,128)}, u32[]{:S(2)}) copy-start(s32[1,64,100]{2,1,0:T(8,128)} %param.23) | copy-start | bytes 76804
  344.5 65.8 %all-gather.6.cloned.1.call-start = ((), (), s32[]{:S(2)}) async-start(), calls=%async_computation.4 | async-start | bytes 2228224 | tf_op jit(solution)/shard_map/all_gather | solution.py:134
  366.5 43.8 %copy-start.1 = (f32[1,64,1024]{2,1,0:T(8,128)S(1)}, f32[1,64,1024]{2,1,0:T(8,128)}, u32[]{:S(2)}) copy-start(f32[1,64,1024]{2,1,0:T(8,128)} %reduce-scatter.2.cloned.1.call-done) | copy-start | bytes 786436
Sparse Core Ops, SparseCore 0:
  10.6 50.5 all-reduce.1
  344.6 21.8 reduce-scatter.1
  369.0 41.2 all-gather.5
Sparse Core Ops, SparseCore 1:
  13.7 101.2 all-gather.3
where the time goes:
time: 514 us; the launch traced here: 506 us
  local copies, waits for them, and re-layouts  267 us (52%)
  waiting for transfers between devices  149 us (29%)
  matrix products  46.2 us (9%)
  other arithmetic  22.3 us (4%)
  between operations  14.8 us (3%)
  starting transfers between devices  7.3 us (1%)
    dynamic_slice x16, local copies, waits for them, and re-layouts, add_block(): taps = lax.dynamic_slice_in_dim(tap_block, base, joined_taps, 0)  59.7 us
    concatenate x8, local copies, waits for them, and re-layouts, add_block(): joined = jnp.concatenate(slabs, axis=-1)  57.2 us
    gather x4, local copies, waits for them, and re-layouts, utterance_loss(): neg_dot = jnp.take_along_axis(scores, neg_ids, axis=1)  48.7 us
    psum x1, waiting for transfers between devices, on_device(): summed = lax.psum(conv_term, 'tensor')  48.5 us
    all_gather x1, waiting for transfers between devices, on_device(): all_targets = lax.all_gather(own_targets, 'seq', axis=1, tiled=True)  41.1 us
    reshape x8, local copies, waits for them, and re-layouts, add_block(): jnp.transpose(taps, (1, 0, 2, 3))  36.6 us
    gather x3, local copies, waits for them, and re-layouts, utterance_loss(): neg_norm = tgt_norm[neg_ids]  35.2 us
    while x8, matrix products  30.8 us
  transfers between devices with their start and end apart: 6, of which 6 were waited for; matrix products, arithmetic and copies ran while one was open for 2% of the time, Pallas kernels for 0%

commit v1 on v0

--- a/solution.py
+++ b/solution.py
@@ -8,6 +8,28 @@
 ln_eps = 1e-05
 norm_eps = 1e-06
 logit_temp = 0.1
+
+
+def joined_along(tiles, dim):
+    tiles = jnp.moveaxis(tiles, 0, dim)
+    shape = tiles.shape
+    return tiles.reshape(*shape[:dim], shape[dim] * shape[dim + 1], *shape[dim + 2 :])
+
+
+def ring_gather(array, axis, dim):
+    count = lax.axis_size(axis)
+    pairs = [(i, (i + 1) % count) for i in range(count)]
+    back = [(b, a) for a, b in pairs]
+    lower, upper = ([], [])
+    for step in range(count - 1):
+        if step % 2 == 0:
+            lower.append(lax.ppermute(lower[-1] if lower else array, axis, pairs))
+        else:
+            upper.append(lax.ppermute(upper[-1] if upper else array, axis, back))
+    parts = jnp.stack([*lower[::-1], array, *upper])
+    shift = lax.axis_index(axis) - len(lower)
+    parts = parts[(jnp.arange(count) - shift) % count]
+    return joined_along(parts, dim)
 
 
 def extended(block, sides, width):
@@ -131,7 +153,7 @@
         tiled=True,
     ).astype(jnp.bfloat16)
     own_targets = make_targets(code_choice, codebook, quant_weight)
-    all_targets = lax.all_gather(own_targets, "seq", axis=1, tiled=True)
+    all_targets = ring_gather(own_targets, "seq", 1)
     is_masked = lax.dynamic_slice_in_dim(masked, lax.axis_index("tensor") * utt_rows, utt_rows, 0)
     return jax.vmap(utterance_loss)(context, own_targets, all_targets, negative_ids, is_masked)
 

time: 514 us -> 535 us (1.041)
  starting transfers between devices: 7.3 us -> 40.1 us
  waiting for transfers between devices: 149 us -> 118 us
  local copies, waits for them, and re-layouts: 267 us -> 285 us
    all_gather x1 -> x0, waiting for transfers between devices: 41.1 us -> none  [on_device(): all_targets = lax.all_gather(own_targets, 'seq', axis=1, tiled=True)]
    ppermute x0 -> x15, starting transfers between devices: none -> 32.8 us  [the longest x7 21.1 us: ring_gather(): upper.append(lax.ppermute(upper[-1] if upper else array, axis, back))]
    unnamed x14 -> x35, local copies, waits for them, and re-layouts: 1.32 us -> 14.9 us
    ppermute x0 -> x15, waiting for transfers between devices: none -> 10.3 us  [the longest x8 9.19 us: ring_gather(): lower.append(lax.ppermute(lower[-1] if lower else array, axis, pairs))]
  transfers between devices with their start and end apart: 6 -> 20, of which waited for: 6 -> 18; matrix products, arithmetic and copies ran while one was open for 2% -> 5% of each run, Pallas kernels for 0% -> 0%
where the time goes in v1:
time: 535 us; the launch traced here: 524 us
  local copies, waits for them, and re-layouts  285 us (53%)
  waiting for transfers between devices  118 us (22%)
  matrix products  43.7 us (8%)
  starting transfers between devices  40.1 us (7%)
  other arithmetic  22.2 us (4%)
  between operations  15.2 us (3%)
    dynamic_slice x16, local copies, waits for them, and re-layouts, add_block(): taps = lax.dynamic_slice_in_dim(tap_block, base, joined_taps, 0)  59.7 us
    concatenate x8, local copies, waits for them, and re-layouts, add_block(): joined = jnp.concatenate(slabs, axis=-1)  57.4 us
    gather x4, local copies, waits for them, and re-layouts, utterance_loss(): neg_dot = jnp.take_along_axis(scores, neg_ids, axis=1)  48.7 us
    psum x1, waiting for transfers between devices, on_device(): summed = lax.psum(conv_term, 'tensor')  48.5 us
    reshape x8, local copies, waits for them, and re-layouts, add_block(): jnp.transpose(taps, (1, 0, 2, 3))  36.8 us
    gather x3, local copies, waits for them, and re-layouts, utterance_loss(): neg_norm = tgt_norm[neg_ids]  35.2 us
    while x8, matrix products  30.7 us
    all_gather x1, waiting for transfers between devices, on_device(): lax.all_gather(pos_weight, ('dp', 'seq'), axis=0, tiled=True)  28.3 us
  transfers between devices with their start and end apart: 20, of which 18 were waited for; matrix products, arithmetic and copies ran while one was open for 5% of the time, Pallas kernels for 0%

profile of v1, /device:TPU:1, one launch (start us, length us, event | category | flops | bytes accessed | tf_op | source)
XLA Modules:
  0.0 524.3 jit_solution(12221575184140428047)
XLA Ops:
  12.7 48.5 %all-reduce.2.cloned.1.call-done = f32[4,64,512]{2,1,0:T(8,128)} async-done(((f32[4,64,512]{2,1,0:T(8,128)}), f32[4,64,512]{2,1,0:T(8,128)}) %all-reduce.2.cloned.1.call-update) | async-done | bytes 524304 | tf_op jit(solution)/shard_map/psum | solution.py:121
  64.9 5.1 collective-permute-start
  72.1 6.6 %collective-permute-done = bf16[4,64,480]{2,1,0:T(8,128)(2,1)S(1)} collective-permute-done((bf16[4,64,480]{2,1,0:T(8,128)(2,1)S(1)}, bf16[4,64,480]{2,1,0:T(8,128)(2,1)S(1)}, u32[]{:S(2)}, u32[]{:S(2)}) %collective-permute-start) | collective-permute-done | bytes 245792 | tf_op jit(solution)/shard_map/ppermute | solution.py:40
  78.7 4.2 collective-permute-done.1
  86.7 28.3 %all-gather.2.cloned.1.call-done = bf16[128,4,120,120]{3,2,1,0:T(8,128)(2,1)} async-done(((bf16[2,4,120,120]{3,2,1,0:T(8,128)(2,1)}), bf16[128,4,120,120]{3,2,1,0:T(8,128)(2,1)}) %all-gather.2.cloned.1.call-update) | async-done | bytes 14745616 | tf_op jit(solution)/shard_map/all_gather | solution.py:142
  114.9 222.8 %while.16 = (s32[]{:T(128)}, f32[4,64,4,120]{3,1,0,2:T(8,128)}, bf16[128,4,120,120]{3,2,1,0:T(8,128)(2,1)}, bf16[4,192,4,120]{3,1,0,2:T(8,128)(2,1)S(1)}, s32[]{...) while((s32[]{:T(128)}, f32[4,64,4,120]{3,1,0,2:T(8,128)}, ...), condition=%wide.region_5.6_spmd.clone, body=%wide.region_4.5_spmd.clone.sunk | while | flops 472105024 | bytes 34530440 | solution.py:97
  117.9 7.2 %concatenate.26 = bf16[4,64,4,1920]{3,1,0,2:T(8,128)(2,1)} concatenate(bf16[4,64,4,120]{3,1,0,2:T(8,128)(2,1)} %get-tuple-element.238, bf16[4,64,4,120]{3,1,0,2:T(8,128)(2,1)} %get-tuple-element.239, bf16[4,64,4,120]{3,1,0,2:T(8,128)(2,1)} %get-tuple-element.240, bf16[4,64,4,120]{3,1,0,2:T(8,128)(2,1)} %get-tuple-element.241, bf16[4,64,4,120]{3,1,0,2:T(8,128)(2,1)} %get-tuple-element.242, ...), dimensions={3} | concatenate | bytes 7864320 | tf_op jit(solution)/shard_map/while/body/eval_jaxpr/concatenate | solution.py:90
  128.1 4.4 copy.47
  132.5 4.6 reshape.374
  137.1 3.8 fusion.190
  144.8 7.2 %concatenate.26 = bf16[4,64,4,1920]{3,1,0,2:T(8,128)(2,1)} concatenate(bf16[4,64,4,120]{3,1,0,2:T(8,128)(2,1)} %get-tuple-element.238, bf16[4,64,4,120]{3,1,0,2:T(8,128)(2,1)} %get-tuple-element.239, bf16[4,64,4,120]{3,1,0,2:T(8,128)(2,1)} %get-tuple-element.240, bf16[4,64,4,120]{3,1,0,2:T(8,128)(2,1)} %get-tuple-element.241, bf16[4,64,4,120]{3,1,0,2:T(8,128)(2,1)} %get-tuple-element.242, ...), dimensions={3} | concatenate | bytes 7864320 | tf_op jit(solution)/shard_map/while/body/eval_jaxpr/concatenate | solution.py:90
  155.0 4.4 copy.47
  159.5 4.6 reshape.374
  164.1 3.8 fusion.190
  172.8 7.2 %concatenate.26 = bf16[4,64,4,1920]{3,1,0,2:T(8,128)(2,1)} concatenate(bf16[4,64,4,120]{3,1,0,2:T(8,128)(2,1)} %get-tuple-element.238, bf16[4,64,4,120]{3,1,0,2:T(8,128)(2,1)} %get-tuple-element.239, bf16[4,64,4,120]{3,1,0,2:T(8,128)(2,1)} %get-tuple-element.240, bf16[4,64,4,120]{3,1,0,2:T(8,128)(2,1)} %get-tuple-element.241, bf16[4,64,4,120]{3,1,0,2:T(8,128)(2,1)} %get-tuple-element.242, ...), dimensions={3} | concatenate | bytes 7864320 | tf_op jit(solution)/shard_map/while/body/eval_jaxpr/concatenate | solution.py:90
  183.0 4.4 copy.47
  187.5 4.6 reshape.374
  192.1 3.8 fusion.190
  200.8 7.2 %concatenate.26 = bf16[4,64,4,1920]{3,1,0,2:T(8,128)(2,1)} concatenate(bf16[4,64,4,120]{3,1,0,2:T(8,128)(2,1)} %get-tuple-element.238, bf16[4,64,4,120]{3,1,0,2:T(8,128)(2,1)} %get-tuple-element.239, bf16[4,64,4,120]{3,1,0,2:T(8,128)(2,1)} %get-tuple-element.240, bf16[4,64,4,120]{3,1,0,2:T(8,128)(2,1)} %get-tuple-element.241, bf16[4,64,4,120]{3,1,0,2:T(8,128)(2,1)} %get-tuple-element.242, ...), dimensions={3} | concatenate | bytes 7864320 | tf_op jit(solution)/shard_map/while/body/eval_jaxpr/concatenate | solution.py:90
  211.0 4.4 copy.47
  215.5 4.6 reshape.374
  220.1 3.8 fusion.190
  228.8 7.2 %concatenate.26 = bf16[4,64,4,1920]{3,1,0,2:T(8,128)(2,1)} concatenate(bf16[4,64,4,120]{3,1,0,2:T(8,128)(2,1)} %get-tuple-element.238, bf16[4,64,4,120]{3,1,0,2:T(8,128)(2,1)} %get-tuple-element.239, bf16[4,64,4,120]{3,1,0,2:T(8,128)(2,1)} %get-tuple-element.240, bf16[4,64,4,120]{3,1,0,2:T(8,128)(2,1)} %get-tuple-element.241, bf16[4,64,4,120]{3,1,0,2:T(8,128)(2,1)} %get-tuple-element.242, ...), dimensions={3} | concatenate | bytes 7864320 | tf_op jit(solution)/shard_map/while/body/eval_jaxpr/concatenate | solution.py:90
  239.0 4.4 copy.47
  243.4 4.6 reshape.374
  248.0 3.8 fusion.190
  256.8 7.2 %concatenate.26 = bf16[4,64,4,1920]{3,1,0,2:T(8,128)(2,1)} concatenate(bf16[4,64,4,120]{3,1,0,2:T(8,128)(2,1)} %get-tuple-element.238, bf16[4,64,4,120]{3,1,0,2:T(8,128)(2,1)} %get-tuple-element.239, bf16[4,64,4,120]{3,1,0,2:T(8,128)(2,1)} %get-tuple-element.240, bf16[4,64,4,120]{3,1,0,2:T(8,128)(2,1)} %get-tuple-element.241, bf16[4,64,4,120]{3,1,0,2:T(8,128)(2,1)} %get-tuple-element.242, ...), dimensions={3} | concatenate | bytes 7864320 | tf_op jit(solution)/shard_map/while/body/eval_jaxpr/concatenate | solution.py:90
  267.0 4.4 copy.47
  271.4 4.6 reshape.374
  276.0 3.8 fusion.190
  284.7 7.2 %concatenate.26 = bf16[4,64,4,1920]{3,1,0,2:T(8,128)(2,1)} concatenate(bf16[4,64,4,120]{3,1,0,2:T(8,128)(2,1)} %get-tuple-element.238, bf16[4,64,4,120]{3,1,0,2:T(8,128)(2,1)} %get-tuple-element.239, bf16[4,64,4,120]{3,1,0,2:T(8,128)(2,1)} %get-tuple-element.240, bf16[4,64,4,120]{3,1,0,2:T(8,128)(2,1)} %get-tuple-element.241, bf16[4,64,4,120]{3,1,0,2:T(8,128)(2,1)} %get-tuple-element.242, ...), dimensions={3} | concatenate | bytes 7864320 | tf_op jit(solution)/shard_map/while/body/eval_jaxpr/concatenate | solution.py:90
  295.0 4.4 copy.47
  299.4 4.6 reshape.374
  304.0 3.8 fusion.190
  312.7 7.2 %concatenate.26 = bf16[4,64,4,1920]{3,1,0,2:T(8,128)(2,1)} concatenate(bf16[4,64,4,120]{3,1,0,2:T(8,128)(2,1)} %get-tuple-element.238, bf16[4,64,4,120]{3,1,0,2:T(8,128)(2,1)} %get-tuple-element.239, bf16[4,64,4,120]{3,1,0,2:T(8,128)(2,1)} %get-tuple-element.240, bf16[4,64,4,120]{3,1,0,2:T(8,128)(2,1)} %get-tuple-element.241, bf16[4,64,4,120]{3,1,0,2:T(8,128)(2,1)} %get-tuple-element.242, ...), dimensions={3} | concatenate | bytes 7864320 | tf_op jit(solution)/shard_map/while/body/eval_jaxpr/concatenate | solution.py:90
  323.0 4.4 copy.47
  327.4 4.6 reshape.374
  332.0 3.8 fusion.190
  340.9 3.8 fusion.4
  347.1 19.2 %reduce-scatter.2.cloned.1.call-done = f32[1,64,1024]{2,1,0:T(8,128)} async-done(((f32[4,64,1024]{2,1,0:T(8,128)}), f32[1,64,1024]{2,1,0:T(8,128)}) %reduce-scatter.2.cloned.1.call-update) | async-done | bytes 262160 | tf_op jit(solution)/shard_map/reduce_scatter | solution.py:149
  368.0 3.6 collective-permute-start.2
  389.4 3.5 collective-permute-start.13
  393.9 4.7 collective-permute-start.14
  400.0 4.7 collective-permute-start.15
  406.0 4.6 collective-permute-start.16
  425.7 3.6 gather_fusion
  432.3 48.5 %gather_fusion.1 = f32[6400]{0:T(1024)S(1)} fusion(f32[1,64,1024]{2,1,0:T(8,128)S(1)} %convolution_bitcast_fusion, s32[6400]{0:T(1024)S(1)} %reshape.336), kind=kCustom, calls=%fused_computation.1 | custom fusion | bytes 128000 | tf_op jit(solution)/shard_map/vmap(jit(take_along_axis))/gather | solution.py:69
  480.9 35.1 %gather_fusion.2 = f32[6400]{0:T(1024)S(1)} fusion(f32[1,1024]{1,0:T(1,128)S(1)} %bitcast.120, s32[6400]{0:T(1024)S(1)} %reshape.344), kind=kCustom, calls=%fused_computation.2 | custom fusion | bytes 102400 | tf_op jit(solution)/shard_map/vmap()/gather | solution.py:70
  (130 shorter events, 124.6 us)
Async XLA Ops:
  7.4 359.0 %copy-start = (bf16[1024,1024]{1,0:T(8,128)(2,1)S(1)}, bf16[1024,1024]{1,0:T(8,128)(2,1)}, u32[]{:S(2)}) copy-start(bf16[1024,1024]{1,0:T(8,128)(2,1)} %param.20) | copy-start | bytes 6291460
  7.4 55.1 %copy-start.7 = (bf16[512,480]{0,1:T(8,128)(2,1)S(1)}, bf16[512,480]{0,1:T(8,128)(2,1)}, u32[]{:S(2)}) copy-start(bf16[512,480]{0,1:T(8,128)(2,1)} %param.15) | copy-start | bytes 1474564
  7.4 55.1 %copy-start.8 = (bf16[480]{0:T(512)(128)(2,1)S(1)}, bf16[480]{0:T(512)(128)(2,1)}, u32[]{:S(2)}) copy-start(bf16[480]{0:T(512)(128)(2,1)} %param.16) | copy-start | bytes 2884
  7.4 53.9 %all-reduce.2.cloned.1.call-start = ((), (), s32[]{:S(2)}) async-start(), calls=%async_computation.1 | async-start | bytes 1048576 | tf_op jit(solution)/shard_map/psum | solution.py:121
  10.5 104.4 %all-gather.2.cloned.1.call-start = ((), (), s32[]{:S(2)}) async-start(), calls=%async_computation.2 | async-start | bytes 15974400 | tf_op jit(solution)/shard_map/all_gather | solution.py:142
  11.1 355.3 %reduce-scatter.2.cloned.1.call-start = ((), (), s32[]{:S(2)}) async-start(), calls=%async_computation.3 | async-start | bytes 1310720 | tf_op jit(solution)/shard_map/reduce_scatter | solution.py:149
  64.9 21.7 %copy-start.3 = (bf16[4,64,480]{2,1,0:T(8,128)(2,1)}, bf16[4,64,480]{2,1,0:T(8,128)(2,1)S(1)}, u32[]{:S(2)}) copy-start(bf16[4,64,480]{2,1,0:T(8,128)(2,1)S(1)} %fusion.1) | copy-start | bytes 737284
  64.9 13.8 %collective-permute-start = (bf16[4,64,480]{2,1,0:T(8,128)(2,1)S(1)}, bf16[4,64,480]{2,1,0:T(8,128)(2,1)S(1)}, u32[]{:S(2)}, u32[]{:S(2)}) collective-permute-start(bf16[4,64,480]{2,1,0:T(8,128)(2,1)S(1)} %fusion.1), channel_id=1, source_target_pairs={{0,4},{4,8},{8,12},{12,16},{16,20},{20,24},{24,28},{28,32},{32,36}... | collective-permute-start | bytes 737288 | tf_op jit(solution)/shard_map/ppermute | solution.py:40
  70.0 12.9 %collective-permute-start.1 = (bf16[4,64,480]{2,1,0:T(8,128)(2,1)S(1)}, bf16[4,64,480]{2,1,0:T(8,128)(2,1)}, u32[]{:S(2)}, u32[]{:S(2)}) collective-permute-start(bf16[4,64,480]{2,1,0:T(8,128)(2,1)S(1)} %fusion.1), channel_id=1, source_target_pairs={{4,0},{8,4},{12,8},{16,12},{20,16},{24,20},{28,24},{32,28},{36,32}... | collective-permute-start | bytes 737288 | tf_op jit(solution)/shard_map/ppermute | solution.py:43
  338.9 2.0 copy-start.4
  340.9 3.8 copy-start.6
  344.7 35.7 %copy-start.5 = (s32[1,64,100]{2,1,0:T(8,128)S(1)}, s32[1,64,100]{2,1,0:T(8,128)}, u32[]{:S(2)}) copy-start(s32[1,64,100]{2,1,0:T(8,128)} %param.23) | copy-start | bytes 76804
  368.0 5.5 %collective-permute-start.2 = (bf16[1,64,1024]{2,1,0:T(8,128)(2,1)S(1)}, bf16[1,64,1024]{2,1,0:T(8,128)(2,1)S(1)}, u32[]{:S(2)}, u32[]{:S(2)}) collective-permute-start(bf16[1,64,1024]{2,1,0:T(8,128)(2,1)S(1)} %bitcast.125), channel_id=1, source_target_pairs={{0,4},{4,8},{8,12},{12,16},{16,20},{20,24},{24,28},{28,32},{32,36}... | collective-permute-start | bytes 393224 | tf_op jit(solution)/shard_map/ppermute | solution.py:26
  373.5 4.4 collective-permute-start.3
  375.9 4.7 collective-permute-start.10
  377.9 4.6 collective-permute-start.4
  380.6 4.4 collective-permute-start.11
  382.5 5.6 %collective-permute-start.5 = (bf16[1,64,1024]{2,1,0:T(8,128)(2,1)S(1)}, bf16[1,64,1024]{2,1,0:T(8,128)(2,1)S(1)}, u32[]{:S(2)}, u32[]{:S(2)}) collective-permute-start(bf16[1,64,1024]{2,1,0:T(8,128)(2,1)S(1)} %collective-permute-done.4), channel_id=1, source_target_pairs={{0,4},{4,8},{8,12},{12,16},{16,20},{20,24},{24,28},{28,32},{32,36}... | collective-permute-start | bytes 393224 | tf_op jit(solution)/shard_map/ppermute | solution.py:26
  385.0 4.4 collective-permute-start.12
  388.1 5.7 %collective-permute-start.6 = (bf16[1,64,1024]{2,1,0:T(8,128)(2,1)S(1)}, bf16[1,64,1024]{2,1,0:T(8,128)(2,1)}, u32[]{:S(2)}, u32[]{:S(2)}) collective-permute-start(bf16[1,64,1024]{2,1,0:T(8,128)(2,1)S(1)} %collective-permute-done.5), channel_id=1, source_target_pairs={{0,4},{4,8},{8,12},{12,16},{16,20},{20,24},{24,28},{28,32},{32,36}... | collective-permute-start | bytes 393224 | tf_op jit(solution)/shard_map/ppermute | solution.py:26
  389.4 4.5 collective-permute-start.13
  393.9 5.9 %collective-permute-start.7 = (bf16[1,64,1024]{2,1,0:T(8,128)(2,1)}, bf16[1,64,1024]{2,1,0:T(8,128)(2,1)}, u32[]{:S(2)}, u32[]{:S(2)}) collective-permute-start(bf16[1,64,1024]{2,1,0:T(8,128)(2,1)} %collective-permute-done.6), channel_id=1, source_target_pairs={{0,4},{4,8},{8,12},{12,16},{16,20},{20,24},{24,28},{28,32},{32,36}... | collective-permute-start | bytes 393224 | tf_op jit(solution)/shard_map/ppermute | solution.py:26
  393.9 6.1 %collective-permute-start.14 = (bf16[1,64,1024]{2,1,0:T(8,128)(2,1)S(1)}, bf16[1,64,1024]{2,1,0:T(8,128)(2,1)}, u32[]{:S(2)}, u32[]{:S(2)}) collective-permute-start(bf16[1,64,1024]{2,1,0:T(8,128)(2,1)S(1)} %collective-permute-done.13), channel_id=1, source_target_pairs={{4,0},{8,4},{12,8},{16,12},{20,16},{24,20},{28,24},{32,28},{36,32}... | collective-permute-start | bytes 393224 | tf_op jit(solution)/shard_map/ppermute | solution.py:28
  399.8 5.9 %collective-permute-start.8 = (bf16[1,64,1024]{2,1,0:T(8,128)(2,1)}, bf16[1,64,1024]{2,1,0:T(8,128)(2,1)}, u32[]{:S(2)}, u32[]{:S(2)}) collective-permute-start(bf16[1,64,1024]{2,1,0:T(8,128)(2,1)} %collective-permute-done.7), channel_id=1, source_target_pairs={{0,4},{4,8},{8,12},{12,16},{16,20},{20,24},{24,28},{28,32},{32,36}... | collective-permute-start | bytes 393224 | tf_op jit(solution)/shard_map/ppermute | solution.py:26
  400.0 5.9 %collective-permute-start.15 = (bf16[1,64,1024]{2,1,0:T(8,128)(2,1)}, bf16[1,64,1024]{2,1,0:T(8,128)(2,1)S(1)}, u32[]{:S(2)}, u32[]{:S(2)}) collective-permute-start(bf16[1,64,1024]{2,1,0:T(8,128)(2,1)} %collective-permute-done.14), channel_id=1, source_target_pairs={{4,0},{8,4},{12,8},{16,12},{20,16},{24,20},{28,24},{32,28},{36,32}... | collective-permute-start | bytes 393224 | tf_op jit(solution)/shard_map/ppermute | solution.py:28
  405.7 5.8 %collective-permute-start.9 = (bf16[1,64,1024]{2,1,0:T(8,128)(2,1)}, bf16[1,64,1024]{2,1,0:T(8,128)(2,1)S(1)}, u32[]{:S(2)}, u32[]{:S(2)}) collective-permute-start(bf16[1,64,1024]{2,1,0:T(8,128)(2,1)} %collective-permute-done.8), channel_id=1, source_target_pairs={{0,4},{4,8},{8,12},{12,16},{16,20},{20,24},{24,28},{28,32},{32,36}... | collective-permute-start | bytes 393224 | tf_op jit(solution)/shard_map/ppermute | solution.py:26
  406.0 19.1 %collective-permute-start.16 = (bf16[1,64,1024]{2,1,0:T(8,128)(2,1)S(1)}, bf16[1,64,1024]{2,1,0:T(8,128)(2,1)S(1)}, u32[]{:S(2)}, u32[]{:S(2)}) collective-permute-start(bf16[1,64,1024]{2,1,0:T(8,128)(2,1)S(1)} %collective-permute-done.15), channel_id=1, source_target_pairs={{4,0},{8,4},{12,8},{16,12},{20,16},{24,20},{28,24},{32,28},{36,32}... | collective-permute-start | bytes 393224 | tf_op jit(solution)/shard_map/ppermute | solution.py:28
  425.7 5.9 %copy-start.2 = (f32[1,64,1024]{2,1,0:T(8,128)S(1)}, f32[1,64,1024]{2,1,0:T(8,128)}, u32[]{:S(2)}) copy-start(f32[1,64,1024]{2,1,0:T(8,128)} %reduce-scatter.2.cloned.1.call-done) | copy-start | bytes 786436
  429.3 2.2 copy-start.1
Sparse Core Ops, SparseCore 0:
  10.6 50.5 all-reduce.1
  344.8 21.5 reduce-scatter.1
Sparse Core Ops, SparseCore 1:
  13.7 101.2 all-gather.1
